TPU v7x, 128 devices: a whole 4x4x4 slice. The times are simulated.
128 devices in a mesh: dp: 16 (over x_lo, z, core), tensor: 8 (over y, x_hi).
Axes of the slice: x: 4 (x_hi: 2, x_lo: 2; x = x_hi * 2 + x_lo), y: 4, z: 4, core: 2. Of those that a mesh axis runs over, the one named last changes fastest.
Arguments:
- tokens: bfloat16 [16384, 1024], P('dp'), may hold values from -6 to 6
- segment_ids: int32 [16384], P('dp'), may hold values from 0 to 7, as said below
- attn_gain: float32 [1024], replicated, may hold values from 0.25 to 1.75
- w_query: bfloat16 [1024, 1024], P(None, 'tensor'), may hold values from -0.1875 to 0.1875
- w_key: bfloat16 [1024, 512], P(None, 'tensor'), may hold values from -0.1875 to 0.1875
- w_value: bfloat16 [1024, 512], P(None, 'tensor'), may hold values from -0.1875 to 0.1875
- query_gain: float32 [64], replicated, may hold values from 0.25 to 1.75
- key_gain: float32 [64], replicated, may hold values from 0.25 to 1.75
- w_out: bfloat16 [1024, 1024], P('tensor'), may hold values from -1.5 to 1.5
- ffn_gain: float32 [1024], replicated, may hold values from 0.25 to 1.75
- w_gate: bfloat16 [1024, 4608], P(None, 'tensor'), may hold values from -0.1875 to 0.1875
- w_up: bfloat16 [1024, 4608], P(None, 'tensor'), may hold values from -0.1875 to 0.1875
- w_down: bfloat16 [4608, 1024], P('tensor'), may hold values from -0.1875 to 0.1875
- cotangent: bfloat16 [16384, 1024], P('dp'), may hold values from -6 to 6
Outputs:
- output: bfloat16 [16384, 1024], P('dp')
- input_grad: float32 [16384, 1024], P('dp')
- attn_gain_grad: float32 [1024], replicated
- w_query_grad: float32 [1024, 1024], P(None, 'tensor')
- w_key_grad: float32 [1024, 512], P(None, 'tensor')
- w_value_grad: float32 [1024, 512], P(None, 'tensor')
- query_gain_grad: float32 [64], replicated
- key_gain_grad: float32 [64], replicated
- w_out_grad: float32 [1024, 1024], P('tensor')
- ffn_gain_grad: float32 [1024], replicated
- w_gate_grad: float32 [1024, 4608], P(None, 'tensor')
- w_up_grad: float32 [1024, 4608], P(None, 'tensor')
- w_down_grad: float32 [4608, 1024], P('tensor')
Inputs may be any that keep to these rules, and one draw needn't show every extreme that they name: `segment_ids`: within each index of dp's 1024 tokens the ids start at 0 and never fall; a sequence is a run of equal ids and never crosses devices.
All inputs are finite; a program needn't handle non-finite values.
Results may differ from a plain program's by a relative error of at most 0.014.
The roundings to bfloat16 on the way count: a program that leaves them out, or rounds other values in their place, can miss the bound.
Values sent between devices are 32-bit elements; how exact they have to be, the bound alone decides.
No kernel may reach another device: no remote copies, remote signals or barrier semaphores. Data moves between devices by JAX's collectives and lax.ppermute only.
A program may use at most 128 MiB of HBM per device.

v0:
```python
import math
import jax
import jax.numpy as jnp
from jax import lax
from jax.sharding import PartitionSpec as P

EPS = 1e-05
THETA = 1000000.0


def outer(first_op, second_op):
    return lax.dot_general(
        first_op, second_op, (((0,), (0,)), ((), ())), preferred_element_type=jnp.float32
    )


def inner(first_op, second_op):
    return lax.dot_general(
        first_op, second_op, (((1,), (1,)), ((), ())), preferred_element_type=jnp.float32
    )


def rms_scale(values):
    return lax.rsqrt(jnp.mean(values * values, axis=-1, keepdims=True) + EPS)


def rms_back(upstream, values, inv_rms, gain_vec):
    normed = values * inv_rms
    weighted = upstream * gain_vec
    return inv_rms * (weighted - normed * jnp.mean(weighted * normed, axis=-1, keepdims=True))


def seq_layout(segment):
    length = segment.shape[0]
    ordinal = jnp.arange(length, dtype=jnp.int32)
    same_seq = segment[:, None] == segment[None, :]
    places = jnp.sum((same_seq & (ordinal[None, :] < ordinal[:, None])).astype(jnp.int32), axis=1)
    allowed = same_seq & (ordinal[None, :] <= ordinal[:, None])
    return (places, allowed)


def rope_tables(places, head_size):
    frequency = jnp.exp(
        jnp.arange(head_size // 2, dtype=jnp.float32) * (-2.0 * math.log(THETA) / head_size)
    )
    angles = places.astype(jnp.float32)[:, None] * frequency[None, :]
    angles = jnp.concatenate([angles, angles], axis=1)
    return (jnp.cos(angles), jnp.sin(angles))


def rotate(values, cosine, sine_table):
    half = values.shape[-1] // 2
    turned = jnp.concatenate([-values[..., half:], values[..., :half]], axis=-1)
    return values * cosine[:, None, :] + turned * sine_table[:, None, :]


def unrotate(incoming, cosine, sine_table):
    half = incoming.shape[-1] // 2
    scaled = incoming * sine_table[:, None, :]
    swapped = jnp.concatenate([scaled[..., half:], -scaled[..., :half]], axis=-1)
    return incoming * cosine[:, None, :] + swapped


def score_table(q_rot, k_rot, allowed, factor):
    raw = jnp.einsum("ikgd,jkd->kgij", q_rot, k_rot, preferred_element_type=jnp.float32) * factor
    return jnp.where(allowed[None, None], raw, -1e30)


def per_device(
    tokens,
    segment_ids,
    attn_gain,
    w_query,
    w_key,
    w_value,
    query_gain,
    key_gain,
    w_out,
    ffn_gain,
    w_gate,
    w_up,
    w_down,
    cotangent,
):
    length = tokens.shape[0]
    head_size = query_gain.shape[0]
    q_heads = w_query.shape[1] // head_size
    kv_heads = w_key.shape[1] // head_size
    groups = q_heads // kv_heads
    factor = 1.0 / math.sqrt(head_size)
    places, allowed = seq_layout(segment_ids)
    cosine, sine_table = rope_tables(places, head_size)
    tokens_wide = tokens.astype(jnp.float32)
    scale_one = rms_scale(tokens_wide)
    normed_one = (tokens_wide * scale_one * attn_gain).astype(jnp.bfloat16)
    q_raw = jnp.dot(normed_one, w_query, preferred_element_type=jnp.float32).reshape(
        length, q_heads, head_size
    )
    k_raw = jnp.dot(normed_one, w_key, preferred_element_type=jnp.float32).reshape(
        length, kv_heads, head_size
    )
    v_half = (
        jnp.dot(normed_one, w_value, preferred_element_type=jnp.float32)
        .astype(jnp.bfloat16)
        .reshape(length, kv_heads, head_size)
    )
    q_scale = rms_scale(q_raw)
    k_scale = rms_scale(k_raw)
    q_hat = q_raw * q_scale
    k_hat = k_raw * k_scale
    q_rot = (
        rotate(q_hat * query_gain, cosine, sine_table)
        .astype(jnp.bfloat16)
        .reshape(length, kv_heads, groups, head_size)
    )
    k_rot = rotate(k_hat * key_gain, cosine, sine_table).astype(jnp.bfloat16)
    scores = score_table(q_rot, k_rot, allowed, factor)
    row_peak = jnp.max(scores, axis=-1, keepdims=True)
    log_total = row_peak + jnp.log(jnp.sum(jnp.exp(scores - row_peak), axis=-1, keepdims=True))
    attn_probs = jnp.exp(scores - log_total).astype(jnp.bfloat16)
    attn_mixed = jnp.einsum(
        "kgij,jkd->ikgd", attn_probs, v_half, preferred_element_type=jnp.float32
    )
    attn_mixed = attn_mixed.reshape(length, q_heads * head_size).astype(jnp.bfloat16)
    attn_sum = lax.psum(jnp.dot(attn_mixed, w_out, preferred_element_type=jnp.float32), "tensor")
    residual = tokens_wide + attn_sum
    scale_two = rms_scale(residual)
    normed_two = (residual * scale_two * ffn_gain).astype(jnp.bfloat16)
    gate_proj = jnp.dot(normed_two, w_gate, preferred_element_type=jnp.float32)
    up_proj = jnp.dot(normed_two, w_up, preferred_element_type=jnp.float32)
    gate_sigmoid = jax.nn.sigmoid(gate_proj)
    hidden = (gate_proj * gate_sigmoid * up_proj).astype(jnp.bfloat16)
    mlp_sum = lax.psum(jnp.dot(hidden, w_down, preferred_element_type=jnp.float32), "tensor")
    output = (residual + mlp_sum).astype(jnp.bfloat16)
    down_grad = outer(hidden, cotangent)
    hidden_grad = inner(cotangent, w_down)
    gate_grad = (
        hidden_grad * up_proj * gate_sigmoid * (1.0 + gate_proj * (1.0 - gate_sigmoid))
    ).astype(jnp.bfloat16)
    up_grad = (hidden_grad * gate_proj * gate_sigmoid).astype(jnp.bfloat16)
    gate_w_grad = outer(normed_two, gate_grad)
    up_w_grad = outer(normed_two, up_grad)
    normed_two_grad = lax.psum(inner(gate_grad, w_gate) + inner(up_grad, w_up), "tensor")
    ffn_grad = jnp.sum(normed_two_grad * residual * scale_two, axis=0)
    residual_grad = cotangent.astype(jnp.float32) + rms_back(
        normed_two_grad, residual, scale_two, ffn_gain
    )
    residual_half = residual_grad.astype(jnp.bfloat16)
    out_w_grad = outer(attn_mixed, residual_half)
    mixed_grad = (
        inner(residual_half, w_out)
        .astype(jnp.bfloat16)
        .reshape(length, kv_heads, groups, head_size)
    )
    attn_full = jnp.exp(score_table(q_rot, k_rot, allowed, factor) - log_total)
    probs_half = attn_full.astype(jnp.bfloat16)
    value_grad = jnp.einsum(
        "kgij,ikgd->jkd", probs_half, mixed_grad, preferred_element_type=jnp.float32
    ).astype(jnp.bfloat16)
    prob_grad = jnp.einsum("ikgd,jkd->kgij", mixed_grad, v_half, preferred_element_type=jnp.float32)
    row_delta = jnp.sum(attn_full * prob_grad, axis=-1, keepdims=True)
    score_grad = (attn_full * (prob_grad - row_delta) * factor).astype(jnp.bfloat16)
    q_rot_grad = jnp.einsum(
        "kgij,jkd->ikgd", score_grad, k_rot, preferred_element_type=jnp.float32
    ).reshape(length, q_heads, head_size)
    k_rot_grad = jnp.einsum("kgij,ikgd->jkd", score_grad, q_rot, preferred_element_type=jnp.float32)
    q_norm_grad = unrotate(q_rot_grad, cosine, sine_table)
    k_norm_grad = unrotate(k_rot_grad, cosine, sine_table)
    qgain_grad = jnp.sum(q_norm_grad * q_hat, axis=(0, 1))
    kgain_grad = jnp.sum(k_norm_grad * k_hat, axis=(0, 1))
    qgain_grad, kgain_grad = lax.psum((qgain_grad, kgain_grad), ("dp", "tensor"))
    q_grad = (
        rms_back(q_norm_grad, q_raw, q_scale, query_gain)
        .astype(jnp.bfloat16)
        .reshape(length, q_heads * head_size)
    )
    k_grad = (
        rms_back(k_norm_grad, k_raw, k_scale, key_gain)
        .astype(jnp.bfloat16)
        .reshape(length, kv_heads * head_size)
    )
    v_grad = value_grad.reshape(length, kv_heads * head_size)
    query_w_grad = outer(normed_one, q_grad)
    key_w_grad = outer(normed_one, k_grad)
    value_w_grad = outer(normed_one, v_grad)
    normed_one_grad = lax.psum(
        inner(q_grad, w_query) + inner(k_grad, w_key) + inner(v_grad, w_value), "tensor"
    )
    attn_grad = jnp.sum(normed_one_grad * tokens_wide * scale_one, axis=0)
    input_grad = residual_grad + rms_back(normed_one_grad, tokens_wide, scale_one, attn_gain)
    (
        attn_grad,
        query_w_grad,
        key_w_grad,
        value_w_grad,
        out_w_grad,
        ffn_grad,
        gate_w_grad,
        up_w_grad,
        down_grad,
    ) = lax.psum(
        (
            attn_grad,
            query_w_grad,
            key_w_grad,
            value_w_grad,
            out_w_grad,
            ffn_grad,
            gate_w_grad,
            up_w_grad,
            down_grad,
        ),
        "dp",
    )
    return (
        output,
        input_grad,
        attn_grad,
        query_w_grad,
        key_w_grad,
        value_w_grad,
        qgain_grad,
        kgain_grad,
        out_w_grad,
        ffn_grad,
        gate_w_grad,
        up_w_grad,
        down_grad,
    )


def solution(mesh):
    return jax.shard_map(
        per_device,
        mesh=mesh,
        in_specs=(
            P("dp", None),
            P("dp"),
            P(),
            P(None, "tensor"),
            P(None, "tensor"),
            P(None, "tensor"),
            P(),
            P(),
            P("tensor", None),
            P(),
            P(None, "tensor"),
            P(None, "tensor"),
            P("tensor", None),
            P("dp", None),
        ),
        out_specs=(
            P("dp", None),
            P("dp", None),
            P(),
            P(None, "tensor"),
            P(None, "tensor"),
            P(None, "tensor"),
            P(),
            P(),
            P("tensor", None),
            P(),
            P(None, "tensor"),
            P(None, "tensor"),
            P("tensor", None),
        ),
        check_vma=False,
    )
```

profile of v0, /device:TPU:0, one launch (start us, length us, event | category | flops | bytes accessed | tf_op | source)
XLA Modules:
  0.0 972.6 jit_solution(14116732110158789731)
XLA Ops:
  9.1 2.3 compare_and_fusion.1
  11.4 2.1 fusion.15
  23.2 1.9 fusion.33
  29.8 2.0 exponential_reduce_fusion
  33.1 2.4 convolution_convert_fusion.1
  36.2 2.7 fusion.55
  39.6 186.9 %all-reduce.9.cloned.1.call-done = f32[1024,1024]{1,0:T(8,128)} async-done(((f32[1024,1024]{1,0:T(8,128)}), f32[1024,1024]{1,0:T(8,128)}) %all-reduce.9.cloned.1.call-update) | async-done | bytes 4194320 | tf_op jit(solution)/shard_map/psum | solution.py:125
  226.4 3.5 multiply_reduce_fusion.2
  235.8 3.4 multiply_convert_fusion.1
  241.0 3.9 convolution_add_fusion
  245.2 5.1 fusion.58
  250.3 178.7 %all-reduce.11.cloned.1.call-done = f32[1024,1024]{1,0:T(8,128)} async-done(((f32[1024,1024]{1,0:T(8,128)}), f32[1024,1024]{1,0:T(8,128)}) %all-reduce.11.cloned.1.call-update) | async-done | bytes 4194320 | tf_op jit(solution)/shard_map/psum | solution.py:143
  429.0 5.4 multiply_reduce_fusion
  434.4 3.7 multiply_add_fusion
  438.1 1.9 copy-done.5
  441.3 3.0 fusion
  444.3 2.5 fusion.20
  446.8 3.1 fusion.18
  451.3 2.0 fusion.40
  457.1 2.7 add_add_fusion
  459.9 4.9 fusion.66
  464.8 2.8 fusion.67
  467.6 2.8 fusion.63
  476.3 328.4 %all-reduce = (f32[64]{0:T(128)}, f32[64]{0:T(128)}) all-reduce(f32[64]{0:T(128)S(1)} %copy-done.63, f32[64]{0:T(128)S(1)} %get-tuple-element.19), channel_id=1, replica_groups=mesh['dp'=16,'tensor'=8] {'dp','tensor'}, use_global_device_ids=true, to_apply=%region_22.23 | all-reduce | flops 128 | bytes 1024 | tf_op jit(solution)/shard_map/psum | solution.py:171
  804.7 3.6 fusion.17
  808.3 31.5 %all-reduce.1 = (f32[1024]{0:T(1024)}, f32[1024]{0:T(1024)}) all-reduce(f32[1024]{0:T(1024)S(1)} %get-tuple-element.15, f32[1024]{0:T(1024)S(1)} %copy-done.57), channel_id=1, replica_groups=mesh['dp'=16,'tensor'=8] {'dp'}, use_global_device_ids=true, to_apply=%region_17.18 | all-reduce | flops 2048 | bytes 16384 | tf_op jit(solution)/shard_map/psum | solution.py:201
  839.8 5.9 add_convert_fusion
  846.8 2.7 fusion.13
  849.4 102.6 %all-reduce.13.cloned.1.call-done = (f32[1024,128]{1,0:T(8,128)}, f32[1024,64]{0,1:T(8,128)}, f32[1024,64]{0,1:T(8,128)}, f32[128,1024]{1,0:T(8,128)}, f32[1024,...) async-done(((f32[1024,128]{1,0:T(8,128)}, f32[1024,64]{0,1:T(8,128)}, f32[1024,64]{0,1:T(8,128)}, f32[128,1024]{1,0:T(8,128)}, f32[1024,576]{0,1:T(8,128)}, ...) | async-done | bytes 8650768 | tf_op jit(solution)/shard_map/psum | solution.py:201
  952.1 2.0 copy.46
  957.4 1.9 copy.49
  959.3 3.5 copy.50
  (195 shorter events, 45.8 us)
Async XLA Ops:
  7.2 228.4 %copy-start = (bf16[576,1024]{1,0:T(8,128)(2,1)S(1)}, bf16[576,1024]{1,0:T(8,128)(2,1)}, u32[]{:S(2)}) copy-start(bf16[576,1024]{1,0:T(8,128)(2,1)} %param.26) | copy-start | bytes 3538948
  7.2 219.2 %all-reduce.9.cloned.1.call-start = ((), (), s32[]{:S(2)}) async-start(), calls=%async_computation | async-start | bytes 8388608 | tf_op jit(solution)/shard_map/psum | solution.py:125
  7.2 6.3 copy-start.8
  7.3 7.6 copy-start.47
  11.4 4.2 copy-start.58
  13.6 3.8 copy-start.53
  14.9 3.3 copy-start.61
  21.7 6.2 copy-start.10
  25.1 4.6 copy-start.49
  31.8 3.7 copy-start.51
  39.0 390.0 %all-reduce.11.cloned.1.call-start = ((), (), s32[]{:S(2)}) async-start(), calls=%async_computation.1 | async-start | bytes 8388608 | tf_op jit(solution)/shard_map/psum | solution.py:143
  229.9 3.7 copy-start.2
  244.9 559.7 %all-reduce.15.cloned.1.call-start = ((), (), s32[]{:S(2)}) async-start(), calls=%async_computation.3 | async-start | bytes 16777216 | tf_op jit(solution)/shard_map/psum | solution.py:133
  250.3 184.1 %copy-start.55 = (f32[1024]{0:T(1024)S(1)}, f32[1024]{0:T(1024)}, u32[]{:S(2)}) copy-start(f32[1024]{0:T(1024)} %param.23) | copy-start | bytes 12292
  429.0 5.4 copy-start.3
  429.0 11.9 %slice-start = ((s8[8388608]{0:T(1024)(128)(4,1)}), s8[4194304]{0:T(1024)(128)(4,1)S(1)}, s32[]{:S(2)}) async-start(s8[8388608]{0:T(1024)(128)(4,1)} %bitcast.195), calls=%async_computation.4 | async-start | bytes 8388608
  434.4 5.7 copy-start.36
  434.4 6.5 slice-start.1
  446.8 10.3 %copy-start.43 = (bf16[1024,64]{0,1:T(8,128)(2,1)}, bf16[1024,64]{0,1:T(8,128)(2,1)S(1)}, u32[]{:S(2)}) copy-start(bf16[1024,64]{0,1:T(8,128)(2,1)S(1)} %fusion.20) | copy-start | bytes 393220
  459.8 5.0 copy-start.24
  459.8 492.2 %all-reduce.13.cloned.1.call-start = ((), (), s32[]{:S(2)}) async-start(), calls=%async_computation.2 | async-start | bytes 17301504 | tf_op jit(solution)/shard_map/psum | solution.py:201
  459.9 4.9 copy-start.28
  467.6 4.0 copy-start.33
  475.6 329.0 %copy-start.9 = (bf16[1024,1024]{1,0:T(8,128)(2,1)S(1)}, bf16[1024,1024]{1,0:T(8,128)(2,1)}, u32[]{:S(2)}) copy-start(bf16[1024,1024]{1,0:T(8,128)(2,1)} %param.14) | copy-start | bytes 6291460
  475.6 329.0 %copy-start.54 = (f32[1024]{0:T(1024)S(1)}, f32[1024]{0:T(1024)}, u32[]{:S(2)}) copy-start(f32[1024]{0:T(1024)} %copy-done.53) | copy-start | bytes 12292
  475.6 329.0 %copy-start.56 = (f32[1024]{0:T(1024)S(1)}, f32[1024]{0:T(1024)}, u32[]{:S(2)}) copy-start(f32[1024]{0:T(1024)} %param.16) | copy-start | bytes 12292
  475.7 332.6 %copy-start.57 = (f32[1024]{0:T(1024)S(1)}, f32[1024]{0:T(1024)}, u32[]{:S(2)}) copy-start(f32[1024]{0:T(1024)} %get-tuple-element.13) | copy-start | bytes 12292
  839.8 5.9 copy-start.7
  839.8 7.0 copy-start.14
  952.1 10.8 %copy-start.26 = (f32[1024,576]{0,1:T(8,128)S(1)}, f32[1024,576]{0,1:T(8,128)}, u32[]{:S(2)}) copy-start(f32[1024,576]{0,1:T(8,128)} %get-tuple-element.77) | copy-start | bytes 7077892
  959.3 4.9 copy-start.25
  959.3 6.3 copy-start.1
  (41 other events, 81.6 us)
Sparse Core Ops, SparseCore 0:
  39.1 187.2 all-reduce.8
  245.1 183.8 all-reduce.10
  459.9 343.1 all-reduce.14
  807.3 144.7 all-reduce.12
where the time goes:
time: 981 us; the launch traced here: 973 us
  waiting for transfers between devices  468 us (48%)
  blocking collectives  360 us (37%)
  matrix products  55.6 us (6%)
  other arithmetic  48.5 us (5%)
  local copies, waits for them, and re-layouts  24.5 us (2%)
  between operations  15 us (2%)
    psum x1, blocking collectives, per_device(): lax.psum((qgain_grad, kgain_grad), ('dp', 'tensor'))  328 us
    psum x1, waiting for transfers between devices, per_device(): lax.psum(jnp.dot(attn_mixed, w_out, preferred_element_type=jnp.float32),...  187 us
    psum x1, waiting for transfers between devices, per_device(): lax.psum(inner(gate_grad, w_gate) + inner(up_grad, w_up), 'tensor')  179 us
    psum x1, waiting for transfers between devices, per_device(): lax.psum((attn_grad, query_w_grad, key_w_grad, value_w_grad, out_w_grad,...  103 us
    psum x1, blocking collectives, per_device(): lax.psum((attn_grad, query_w_grad, key_w_grad, value_w_grad, out_w_grad,...  31.5 us
    unnamed x145, local copies, waits for them, and re-layouts  22.7 us
  transfers between devices with their start and end apart: 4, of which 3 were waited for; matrix products, arithmetic and copies ran while one was open for 3% of the time, Pallas kernels for 0%

commit v1 on v0

--- a/solution.py
+++ b/solution.py
@@ -122,7 +122,10 @@
         "kgij,jkd->ikgd", attn_probs, v_half, preferred_element_type=jnp.float32
     )
     attn_mixed = attn_mixed.reshape(length, q_heads * head_size).astype(jnp.bfloat16)
-    attn_sum = lax.psum(jnp.dot(attn_mixed, w_out, preferred_element_type=jnp.float32), "tensor")
+    attn_sum = jnp.sum(
+        lax.all_gather(jnp.dot(attn_mixed, w_out, preferred_element_type=jnp.float32), "tensor"),
+        axis=0,
+    )
     residual = tokens_wide + attn_sum
     scale_two = rms_scale(residual)
     normed_two = (residual * scale_two * ffn_gain).astype(jnp.bfloat16)

time: 981 us -> 1140 us (1.16)
  waiting for transfers between devices: 468 us -> 617 us
    all_gather x0 -> x1, waiting for transfers between devices: none -> 336 us  [per_device(): lax.all_gather(jnp.dot(attn_mixed, w_out, preferred_element_type=jnp.floa...]
    psum x1 -> x0, waiting for transfers between devices: 187 us -> none  [per_device(): lax.psum(jnp.dot(attn_mixed, w_out, preferred_element_type=jnp.float32),...]
    reduce_sum x0 -> x1, other arithmetic: none -> 14.7 us  [per_device(): jnp.sum(lax.all_gather(jnp.dot(attn_mixed, w_out, preferred_element_type=...]
    unnamed x145 -> x155, local copies, waits for them, and re-layouts: 22.7 us -> 24.7 us
where the time goes in v1:
time: 1140 us; the launch traced here: 1130 us
  waiting for transfers between devices  617 us (54%)
  blocking collectives  358 us (31%)
  other arithmetic  57.6 us (5%)
  matrix products  55.3 us (5%)
  local copies, waits for them, and re-layouts  25.4 us (2%)
  between operations  15.1 us (1%)
    all_gather x1, waiting for transfers between devices, per_device(): lax.all_gather(jnp.dot(attn_mixed, w_out, preferred_element_type=jnp.floa...  336 us
    psum x1, blocking collectives, per_device(): lax.psum((qgain_grad, kgain_grad), ('dp', 'tensor'))  329 us
    psum x1, waiting for transfers between devices, per_device(): lax.psum(inner(gate_grad, w_gate) + inner(up_grad, w_up), 'tensor')  178 us
    psum x1, waiting for transfers between devices, per_device(): lax.psum((attn_grad, query_w_grad, key_w_grad, value_w_grad, out_w_grad,...  104 us
    psum x1, blocking collectives, per_device(): lax.psum((attn_grad, query_w_grad, key_w_grad, value_w_grad, out_w_grad,...  29.3 us
    unnamed x155, local copies, waits for them, and re-layouts  24.7 us
  transfers between devices with their start and end apart: 4, of which 3 were waited for; matrix products, arithmetic and copies ran while one was open for 3% of the time, Pallas kernels for 0%

profile of v1, /device:TPU:0, one launch (start us, length us, event | category | flops | bytes accessed | tf_op | source)
XLA Modules:
  0.0 1129.6 jit_solution(1236147289378812340)
XLA Ops:
  9.0 2.4 compare_and_fusion.1
  12.1 2.1 fusion.15
  14.2 2.2 fusion.9
  24.0 2.0 exponential_reduce_fusion
  27.2 2.4 convolution_convert_fusion.1
  30.4 2.7 fusion.55
  33.7 336.0 %all-gather.3.cloned.1.call-done = f32[8192,1024]{1,0:T(8,128)} async-done(((f32[1024,1024]{1,0:T(8,128)}), f32[8192,1024]{1,0:T(8,128)}) %all-gather.3.cloned.1.call-update) | async-done | bytes 33554448 | tf_op jit(solution)/shard_map/all_gather | solution.py:126
  369.8 14.7 %reduce_sum.149 = f32[1024,1024]{1,0:T(8,128)} reduce(f32[8,1024,1024]{2,1,0:T(8,128)} %bitcast.198, f32[]{:T(128)} %constant.10.clone.1), dimensions={0}, to_apply=%region_6.7 | reduce | flops 7340032 | bytes 37748740 | tf_op jit(solution)/shard_map/reduce_sum | solution.py:125
  384.4 3.5 multiply_reduce_fusion.2
  393.7 3.3 multiply_convert_fusion.1
  398.9 4.0 convolution_add_fusion
  403.2 5.1 fusion.58
  408.3 177.6 %all-reduce.8.cloned.1.call-done = f32[1024,1024]{1,0:T(8,128)} async-done(((f32[1024,1024]{1,0:T(8,128)}), f32[1024,1024]{1,0:T(8,128)}) %all-reduce.8.cloned.1.call-update) | async-done | bytes 4194320 | tf_op jit(solution)/shard_map/psum | solution.py:146
  585.9 5.4 multiply_reduce_fusion
  591.3 3.7 multiply_add_fusion
  595.0 2.0 copy-done.5
  598.2 2.5 fusion.20
  600.8 3.0 fusion
  603.8 3.1 fusion.18
  608.2 2.0 fusion.40
  614.1 2.7 add_add_fusion
  618.0 4.5 fusion.67
  622.6 2.8 fusion.66
  625.4 2.8 fusion.63
  634.1 328.8 %all-reduce = (f32[64]{0:T(128)}, f32[64]{0:T(128)}) all-reduce(f32[64]{0:T(128)S(1)} %copy-done.67, f32[64]{0:T(128)S(1)} %get-tuple-element.19), channel_id=1, replica_groups=mesh['dp'=16,'tensor'=8] {'dp','tensor'}, use_global_device_ids=true, to_apply=%region_22.23 | all-reduce | flops 128 | bytes 1024 | tf_op jit(solution)/shard_map/psum | solution.py:174
  962.9 3.6 fusion.17
  966.5 29.3 %all-reduce.1 = (f32[1024]{0:T(1024)}, f32[1024]{0:T(1024)}) all-reduce(f32[1024]{0:T(1024)S(1)} %get-tuple-element.15, f32[1024]{0:T(1024)S(1)} %copy-done.59), channel_id=1, replica_groups=mesh['dp'=16,'tensor'=8] {'dp'}, use_global_device_ids=true, to_apply=%region_17.18 | all-reduce | flops 2048 | bytes 16384 | tf_op jit(solution)/shard_map/psum | solution.py:204
  995.8 5.8 add_convert_fusion
  1002.8 2.7 fusion.13
  1005.5 103.6 %all-reduce.10.cloned.1.call-done = (f32[1024,128]{1,0:T(8,128)}, f32[1024,64]{0,1:T(8,128)}, f32[1024,64]{0,1:T(8,128)}, f32[128,1024]{1,0:T(8,128)}, f32[1024,...) async-done(((f32[1024,128]{1,0:T(8,128)}, f32[1024,64]{0,1:T(8,128)}, f32[1024,64]{0,1:T(8,128)}, f32[128,1024]{1,0:T(8,128)}, f32[1024,576]{0,1:T(8,128)}, ...) | async-done | bytes 8650768 | tf_op jit(solution)/shard_map/psum | solution.py:204
  1109.1 2.0 copy.45
  1116.3 3.5 copy.49
  (206 shorter events, 42.7 us)
Async XLA Ops:
  7.2 386.4 %copy-start = (bf16[576,1024]{1,0:T(8,128)(2,1)S(1)}, bf16[576,1024]{1,0:T(8,128)(2,1)}, u32[]{:S(2)}) copy-start(bf16[576,1024]{1,0:T(8,128)(2,1)} %param.26) | copy-start | bytes 3538948
  7.2 9.2 copy-start.42
  7.2 362.6 %all-gather.3.cloned.1.call-start = ((), (), s32[]{:S(2)}) async-start(), calls=%async_computation.1 | async-start | bytes 37748736 | tf_op jit(solution)/shard_map/all_gather | solution.py:126
  12.1 9.2 copy-start.62
  12.1 5.1 copy-start.48
  14.2 3.8 copy-start.54
  14.2 3.8 copy-start.60
  14.2 3.9 copy-start.40
  17.2 8.8 copy-start.44
  18.2 4.0 copy-start.9
  33.1 552.7 %all-reduce.8.cloned.1.call-start = ((), (), s32[]{:S(2)}) async-start(), calls=%async_computation | async-start | bytes 8388608 | tf_op jit(solution)/shard_map/psum | solution.py:146
  387.9 3.6 copy-start.2
  403.0 559.9 %all-reduce.12.cloned.1.call-start = ((), (), s32[]{:S(2)}) async-start(), calls=%async_computation.3 | async-start | bytes 16777216 | tf_op jit(solution)/shard_map/psum | solution.py:136
  408.3 183.0 %copy-start.57 = (f32[1024]{0:T(1024)S(1)}, f32[1024]{0:T(1024)}, u32[]{:S(2)}) copy-start(f32[1024]{0:T(1024)} %param.23) | copy-start | bytes 12292
  585.9 5.4 copy-start.3
  585.9 12.0 %slice-start = ((s8[8388608]{0:T(1024)(128)(4,1)}), s8[4194304]{0:T(1024)(128)(4,1)S(1)}, s32[]{:S(2)}) async-start(s8[8388608]{0:T(1024)(128)(4,1)} %bitcast.196), calls=%async_computation.4 | async-start | bytes 8388608
  591.2 5.7 copy-start.37
  591.3 6.6 slice-start.1
  600.8 13.3 %copy-start.46 = (bf16[1024,64]{0,1:T(8,128)(2,1)}, bf16[1024,64]{0,1:T(8,128)(2,1)S(1)}, u32[]{:S(2)}) copy-start(bf16[1024,64]{0,1:T(8,128)(2,1)S(1)} %fusion.20) | copy-start | bytes 393220
  616.8 492.3 %all-reduce.10.cloned.1.call-start = ((), (), s32[]{:S(2)}) async-start(), calls=%async_computation.2 | async-start | bytes 17301504 | tf_op jit(solution)/shard_map/psum | solution.py:204
  618.0 4.5 copy-start.29
  618.0 4.5 copy-start.71
  625.4 4.0 copy-start.34
  633.5 329.5 %copy-start.8 = (bf16[1024,1024]{1,0:T(8,128)(2,1)S(1)}, bf16[1024,1024]{1,0:T(8,128)(2,1)}, u32[]{:S(2)}) copy-start(bf16[1024,1024]{1,0:T(8,128)(2,1)} %param.14) | copy-start | bytes 6291460
  633.5 329.5 %copy-start.55 = (f32[1024]{0:T(1024)S(1)}, f32[1024]{0:T(1024)}, u32[]{:S(2)}) copy-start(f32[1024]{0:T(1024)} %copy-done.54) | copy-start | bytes 12292
  633.5 329.5 %copy-start.58 = (f32[1024]{0:T(1024)S(1)}, f32[1024]{0:T(1024)}, u32[]{:S(2)}) copy-start(f32[1024]{0:T(1024)} %param.16) | copy-start | bytes 12292
  633.5 333.0 %copy-start.59 = (f32[1024]{0:T(1024)S(1)}, f32[1024]{0:T(1024)}, u32[]{:S(2)}) copy-start(f32[1024]{0:T(1024)} %get-tuple-element.13) | copy-start | bytes 12292
  995.8 5.9 copy-start.7
  995.8 7.0 copy-start.13
  1109.0 10.8 copy-start.27
  1116.3 4.9 copy-start.26
  1116.3 6.3 copy-start.1
  (46 other events, 94.3 us)
Sparse Core Ops, SparseCore 0:
  33.3 336.4 all-gather.2
  403.1 182.7 all-reduce.7
  616.9 343.2 all-reduce.11
  964.3 144.7 all-reduce.9
